TPU v7x, 32 devices: a whole 2x2x4 slice. The times are simulated.
32 devices in a mesh: row: 4 (over y, x), col: 8 (over z, core).
Axes of the slice: x: 2, y: 2, z: 4, core: 2. Of those that a mesh axis runs over, the one named last changes fastest.
Arguments:
- inv_sep: bfloat16 [24576, 24576], P('row', 'col'), may hold values from -6 to 6
- lower_one: bfloat16 [24576, 256], P('col', 'row'), may hold values from -0.078125 to 0.078125
- upper_one: bfloat16 [256, 24576], P('col', 'row'), may hold values from -0.078125 to 0.078125
- diag_inv_one: float32 [256, 256], replicated, may hold values from -6 to 6
- blocks_one: int32 [40], replicated, may hold values from 0 to 191, as said below
- lower_two: bfloat16 [24576, 256], P('col', 'row'), may hold values from -0.09375 to 0.09375
- upper_two: bfloat16 [256, 24576], P('col', 'row'), may hold values from -0.09375 to 0.09375
- corner_lower: bfloat16 [256, 256], replicated, may hold values from -0.375 to 0.375
- corner_upper: bfloat16 [256, 256], replicated, may hold values from -0.375 to 0.375
- diag_inv_two: float32 [256, 256], replicated, may hold values from -6 to 6
- blocks_two: int32 [32], replicated, may hold values from 0 to 191, as said below
Outputs:
- inv_lower_one: bfloat16 [5120, 256], P(('row', 'col'))
- inv_upper_one: bfloat16 [256, 5120], P('row', 'col')
- inv_diag_one: float32 [256, 256], replicated
- inv_lower_two: bfloat16 [4096, 256], P(('row', 'col'))
- inv_upper_two: bfloat16 [256, 4096], P('row', 'col')
- inv_diag_two: float32 [256, 256], replicated
Inputs may be any that keep to these rules, and one draw needn't show every extreme that they name: `blocks_one`: distinct block indices in increasing order; each aligned run of 24 blocks holds exactly 5 of them; the first and the last block of the separator are listed. `blocks_two`: distinct block indices in increasing order, each of them also in blocks_one; each aligned run of 24 blocks holds exactly 4 of them; the first and the last block of the separator are listed.
All inputs are finite; a program needn't handle non-finite values.
Results may differ from a plain program's by a relative error of at most 0.0039.
Values may be sent and summed in bfloat16 or wider, within the bound.
No kernel may reach another device: no remote copies, remote signals or barrier semaphores. Data moves between devices by JAX's collectives and lax.ppermute only.
A program may use at most 128 MiB of HBM per device.

v0:
```python
import jax
import jax.numpy as jnp
from jax import lax
from jax.sharding import PartitionSpec as P

B = 128


def highest(first_mat, second_mat):
    return jnp.dot(
        first_mat.astype(jnp.float32),
        second_mat.astype(jnp.float32),
        precision=lax.Precision.HIGHEST,
    )


def take_rows(matrix, blocks):
    shaped = matrix.reshape(matrix.shape[0] // B, B, matrix.shape[1])
    return jnp.take(shaped, blocks, axis=0).reshape(blocks.shape[0] * B, matrix.shape[1])


def take_cols(matrix, blocks):
    shaped = matrix.reshape(matrix.shape[0], matrix.shape[1] // B, B)
    return jnp.take(shaped, blocks, axis=1).reshape(matrix.shape[0], blocks.shape[0] * B)


def block_rows(blocks):
    return (blocks[:, None] * B + jnp.arange(B, dtype=jnp.int32)[None, :]).reshape(-1)


def places(wanted, listed):
    return jnp.sum((listed[None, :] < wanted[:, None]).astype(jnp.int32), axis=1)


def on_device(
    inv_sep,
    lower_one,
    upper_one,
    diag_inv_one,
    blocks_one,
    lower_two,
    upper_two,
    corner_lower,
    corner_upper,
    diag_inv_two,
    blocks_two,
):
    row_index = lax.axis_index("row")
    col_index = lax.axis_index("col")
    row_count = lax.axis_size("row")
    col_count = lax.axis_size("col")
    rows_here, cols_here = inv_sep.shape
    panel_width = diag_inv_one.shape[0]
    run_blocks = cols_here // B
    pick_one = blocks_one.shape[0] // col_count
    pick_two = blocks_two.shape[0] // col_count
    runs_group = col_count // row_count
    group_one = pick_one * runs_group
    group_two = pick_two * runs_group
    share_one = pick_one * B // row_count
    share_two = pick_two * B // row_count
    upper_rows = panel_width // row_count
    row_one = lax.dynamic_slice_in_dim(blocks_one, row_index * group_one, group_one) - row_index * (
        rows_here // B
    )
    row_two = lax.dynamic_slice_in_dim(blocks_two, row_index * group_two, group_two) - row_index * (
        rows_here // B
    )
    col_one = (
        lax.dynamic_slice_in_dim(blocks_one, col_index * pick_one, pick_one)
        - col_index * run_blocks
    )
    col_two = (
        lax.dynamic_slice_in_dim(blocks_two, col_index * pick_two, pick_two)
        - col_index * run_blocks
    )
    sep_one = take_cols(take_rows(inv_sep, row_one), col_one)
    sep_two = take_cols(take_rows(inv_sep, row_two), col_two)
    lower_spots = block_rows(places(row_two, row_one))
    upper_spots = places(col_two, col_one)
    corner_mine = lax.dynamic_slice_in_dim(corner_upper, row_index * upper_rows, upper_rows, 1)
    lower_p = lax.all_gather(take_rows(lower_one, col_one), "row", axis=1, tiled=True)
    upper_p = lax.all_gather(take_cols(upper_one, row_one), "col", axis=0, tiled=True)
    inv_lower_one = lax.psum_scatter(
        -jnp.dot(sep_one, lower_p, preferred_element_type=jnp.float32),
        "col",
        scatter_dimension=0,
        tiled=True,
    ).astype(jnp.bfloat16)
    inv_upper_one = lax.psum_scatter(
        -jnp.dot(upper_p, sep_one, preferred_element_type=jnp.float32),
        "row",
        scatter_dimension=0,
        tiled=True,
    ).astype(jnp.bfloat16)
    lower_c = lax.all_gather(take_rows(lower_two, col_two), "row", axis=1, tiled=True)
    upper_c = lax.all_gather(take_cols(upper_two, row_two), "col", axis=0, tiled=True)
    own_rows = col_index * share_one + jnp.arange(share_one, dtype=jnp.int32)
    chooser = (lower_spots[:, None] == own_rows[None, :]).astype(jnp.float32)
    carried = jnp.dot(inv_lower_one, corner_lower, preferred_element_type=jnp.float32)
    direct = jnp.dot(sep_two, lower_c, preferred_element_type=jnp.float32)
    shifted_part = jnp.dot(chooser, carried, precision=lax.Precision.HIGHEST)
    inv_lower_two = lax.psum_scatter(
        -(direct + shifted_part), "col", scatter_dimension=0, tiled=True
    ).astype(jnp.bfloat16)
    ancestor_cols = take_cols(inv_upper_one, upper_spots)
    direct = jnp.dot(upper_c, sep_two, preferred_element_type=jnp.float32)
    shifted_part = jnp.dot(corner_mine, ancestor_cols, preferred_element_type=jnp.float32)
    inv_upper_two = lax.psum_scatter(
        -(direct + shifted_part), "row", scatter_dimension=0, tiled=True
    ).astype(jnp.bfloat16)
    upper_slab = lax.dynamic_slice_in_dim(upper_p, col_index * share_one, share_one, 1)
    second_slab = lax.dynamic_slice_in_dim(upper_c, col_index * share_two, share_two, 1)
    first_part = jnp.dot(upper_slab, inv_lower_one, preferred_element_type=jnp.float32)
    cross = jnp.dot(ancestor_cols, lower_c, preferred_element_type=jnp.float32)
    second_part = jnp.dot(second_slab, inv_lower_two, preferred_element_type=jnp.float32) - highest(
        corner_mine, cross
    )
    extra_part = highest(corner_upper, highest(first_part, corner_lower))
    first_total, second_total = lax.psum((first_part, second_part + extra_part), ("row", "col"))
    inv_diag_one = diag_inv_one - first_total
    tail_term = highest(corner_upper, highest(diag_inv_one, corner_lower))
    inv_diag_two = diag_inv_two - (second_total - tail_term)
    return (inv_lower_one, inv_upper_one, inv_diag_one, inv_lower_two, inv_upper_two, inv_diag_two)


def solution(mesh):
    return jax.shard_map(
        on_device,
        mesh=mesh,
        in_specs=(
            P("row", "col"),
            P("col", "row"),
            P("col", "row"),
            P(),
            P(),
            P("col", "row"),
            P("col", "row"),
            P(),
            P(),
            P(),
            P(),
        ),
        out_specs=(
            P(("row", "col"), None),
            P("row", "col"),
            P(),
            P(("row", "col"), None),
            P("row", "col"),
            P(),
        ),
        check_vma=False,
    )
```

profile of v0, /device:TPU:0, one launch (start us, length us, event | category | flops | bytes accessed | tf_op | source)
XLA Modules:
  0.0 326.3 jit_solution(9898332100142515147)
XLA Ops:
  8.0 8.9 %gather_fusion = bf16[10,128,3072]{2,1,0:T(8,128)(2,1)} fusion(bf16[48,128,3072]{2,1,0:T(8,128)(2,1)} %bitcast.126, s32[1024]{0:T(1024)S(1)} %pad_clamp_fusion.4), kind=kCustom, calls=%fused_computation | custom fusion | bytes 15728680 | tf_op jit(solution)/shard_map/jit(_take)/gather | solution.py:19
  16.9 8.3 %copy.69 = bf16[160,8,24,128]{3,2,1,0:T(8,128)(2,1)} copy(bf16[160,8,24,128]{3,1,2,0:T(8,128)(2,1)} %bitcast.121) | data formatting | bytes 15728640
  25.4 8.6 %copy_select_fusion = bf16[1280,24,128]{2,0,1:T(8,128)(2,1)} fusion(bf16[1280,24,128]{2,1,0:T(8,128)(2,1)} %bitcast.122, pred[1280]{0:T(1024)(128)(4,1)S(1)} %broadcast_bitcast_fusion), kind=kLoop, calls=%fused_computation.9 | loop fusion | flops 3932160 | bytes 15729920 | tf_op jit(solution)/shard_map/jit(_take)/select_n | solution.py:19
  34.0 4.1 %gather_fusion.1 = bf16[5,1280,128]{2,1,0:T(8,128)(2,1)S(1)} fusion(bf16[1280,24,128]{2,0,1:T(8,128)(2,1)} %copy_select_fusion, s32[1024]{0:T(1024)S(1)} %pad_clamp_fusion.3), kind=kCustom, calls=%fused_computation.1 | custom fusion | bytes 3276820 | tf_op jit(solution)/shard_map/jit(_take)/gather | solution.py:24
  38.1 2.4 copy.42
  41.2 1.6 bitcast_select_fusion
  42.9 11.0 %all_gather.12 = bf16[640,256]{0,1:T(8,128)(2,1)S(1)} all-gather(bf16[640,64]{0,1:T(8,128)(2,1)S(1)} %bitcast_select_fusion.3), channel_id=1, replica_groups=mesh['row'=4,'col'=8] {'row'}, dimensions={1}, use_global_device_ids=true | all-gather | bytes 409600 | tf_op jit(solution)/shard_map/all_gather | solution.py:82
  53.8 1.8 convolution_negate_fusion
  56.4 17.9 %all_gather.13 = bf16[256,1280]{1,0:T(8,128)(2,1)S(1)} all-gather(bf16[32,1280]{1,0:T(8,128)(2,1)S(1)} %bitcast_select_fusion.2), channel_id=1, replica_groups=mesh['row'=4,'col'=8] {'col'}, dimensions={0}, use_global_device_ids=true | all-gather | bytes 737280 | tf_op jit(solution)/shard_map/all_gather | solution.py:83
  77.2 6.5 %gather_fusion.4 = bf16[8,128,3072]{2,1,0:T(8,128)(2,1)} fusion(bf16[48,128,3072]{2,1,0:T(8,128)(2,1)} %bitcast.127, s32[1024]{0:T(1024)S(1)} %pad_clamp_fusion.2), kind=kCustom, calls=%fused_computation.4 | custom fusion | bytes 12582944 | tf_op jit(solution)/shard_map/jit(_take)/gather | solution.py:19
  83.6 4.8 %copy.70 = bf16[128,8,24,128]{3,2,1,0:T(8,128)(2,1)S(1)} copy(bf16[128,8,24,128]{3,1,2,0:T(8,128)(2,1)} %bitcast.124) | data formatting | bytes 12582912
  88.5 4.2 %copy_select_fusion.1 = bf16[1024,24,128]{2,0,1:T(8,128)(2,1)} fusion(bf16[1024,24,128]{2,1,0:T(8,128)(2,1)S(1)} %bitcast.123, pred[1024]{0:T(1024)(128)(4,1)S(1)} %broadcast_bitcast_fusion.1), kind=kLoop, calls=%fused_computation.10 | loop fusion | flops 3145728 | bytes 12583936 | tf_op jit(solution)/shard_map/jit(_take)/select_n | solution.py:19
  92.7 3.6 %gather_fusion.5 = bf16[4,1024,128]{2,1,0:T(8,128)(2,1)S(1)} fusion(bf16[1024,24,128]{2,0,1:T(8,128)(2,1)} %copy_select_fusion.1, s32[1024]{0:T(1024)S(1)} %pad_clamp_fusion.1), kind=kCustom, calls=%fused_computation.5 | custom fusion | bytes 2097168 | tf_op jit(solution)/shard_map/jit(_take)/gather | solution.py:24
  98.6 9.4 %all_gather.14 = bf16[512,256]{0,1:T(8,128)(2,1)S(1)} all-gather(bf16[512,64]{0,1:T(8,128)(2,1)S(1)} %bitcast_select_fusion.6), channel_id=1, replica_groups=mesh['row'=4,'col'=8] {'row'}, dimensions={1}, use_global_device_ids=true | all-gather | bytes 327680 | tf_op jit(solution)/shard_map/all_gather | solution.py:96
  108.7 1.8 copy_bitcast_fusion
  112.4 1.6 fusion
  114.2 1.6 gather_fusion.7
  115.9 14.9 %all_gather.15 = bf16[256,1024]{1,0:T(8,128)(2,1)S(1)} all-gather(bf16[32,1024]{1,0:T(8,128)(2,1)S(1)} %bitcast_select_fusion.5), channel_id=1, replica_groups=mesh['row'=4,'col'=8] {'col'}, dimensions={0}, use_global_device_ids=true | all-gather | bytes 589824 | tf_op jit(solution)/shard_map/all_gather | solution.py:97
  137.7 16.5 %reduce-scatter.9.cloned.1.call-done = f32[128,256]{1,0:T(8,128)} async-done(((f32[1024,256]{1,0:T(8,128)}), f32[128,256]{1,0:T(8,128)}) %reduce-scatter.9.cloned.1.call-update) | async-done | bytes 131088 | tf_op jit(solution)/shard_map/reduce_scatter | solution.py:103
  156.5 1.9 fusion.4
  160.3 20.3 %reduce-scatter.11.cloned.1.call-done = f32[64,512]{1,0:T(8,128)} async-done(((f32[256,512]{1,0:T(8,128)}), f32[64,512]{1,0:T(8,128)}) %reduce-scatter.11.cloned.1.call-update) | async-done | bytes 131088 | tf_op jit(solution)/shard_map/reduce_scatter | solution.py:109
  182.2 133.7 %all-reduce.3.cloned.1.call-done = (f32[256,256]{1,0:T(8,128)}, f32[256,256]{1,0:T(8,128)}) async-done(((f32[256,256]{1,0:T(8,128)}, f32[256,256]{1,0:T(8,128)}), (f32[256,256]{1,0:T(8,128)}, f32[256,256]{1,0:T(8,128)})) %all-reduce.3.cloned.1.call-update) | async-done | bytes 524304 | tf_op jit(solution)/shard_map/psum | solution.py:120
  315.9 1.8 sub.40
  317.7 2.1 fusion.3
  (88 shorter events, 23.0 us)
Async XLA Ops:
  7.2 33.4 %copy-start = (bf16[3072,64]{0,1:T(8,128)(2,1)S(1)}, bf16[3072,64]{0,1:T(8,128)(2,1)}, u32[]{:S(2)}) copy-start(bf16[3072,64]{0,1:T(8,128)(2,1)} %param.12) | copy-start | bytes 1179652
  7.2 104.1 %reduce-scatter.5.cloned.1.call-start = ((), (), s32[]{:S(2)}) async-start(), calls=%async_computation.4 | async-start | bytes 1474560 | tf_op jit(solution)/shard_map/reduce_scatter | solution.py:84
  16.9 8.3 %copy-start.9 = (s32[40]{0:T(128)S(1)}, s32[40]{0:T(128)}, u32[]{:S(2)}) copy-start(s32[40]{0:T(128)} %param.15) | copy-start | bytes 484
  40.4 15.3 %copy-start.7 = (bf16[32,6144]{1,0:T(8,128)(2,1)S(1)}, bf16[32,6144]{1,0:T(8,128)(2,1)}, u32[]{:S(2)}) copy-start(bf16[32,6144]{1,0:T(8,128)(2,1)} %param.13) | copy-start | bytes 1179652
  53.8 22.3 %copy-start.10 = (s32[32]{0:T(128)S(1)}, s32[32]{0:T(128)}, u32[]{:S(2)}) copy-start(s32[32]{0:T(128)} %param.21) | copy-start | bytes 388
  55.7 75.1 %reduce-scatter.7.cloned.1.call-start = ((), (), s32[]{:S(2)}) async-start(), calls=%async_computation.5 | async-start | bytes 819200 | tf_op jit(solution)/shard_map/reduce_scatter | solution.py:90
  75.9 78.3 %reduce-scatter.9.cloned.1.call-start = ((), (), s32[]{:S(2)}) async-start(), calls=%async_computation.6 | async-start | bytes 1179648 | tf_op jit(solution)/shard_map/reduce_scatter | solution.py:103
  92.7 19.5 %copy-start.3 = (bf16[256,256]{1,0:T(8,128)(2,1)S(1)}, bf16[256,256]{1,0:T(8,128)(2,1)}, u32[]{:S(2)}) copy-start(bf16[256,256]{1,0:T(8,128)(2,1)} %param.18) | copy-start | bytes 393220
  112.3 1.8 copy-start.4
  114.1 205.7 %copy-start.1 = (bf16[3072,64]{0,1:T(8,128)(2,1)S(1)}, bf16[3072,64]{0,1:T(8,128)(2,1)}, u32[]{:S(2)}) copy-start(bf16[3072,64]{0,1:T(8,128)(2,1)} %param.12) | copy-start | bytes 1179652
  114.1 66.5 %reduce-scatter.11.cloned.1.call-start = ((), (), s32[]{:S(2)}) async-start(), calls=%async_computation.7 | async-start | bytes 655360 | tf_op jit(solution)/shard_map/reduce_scatter | solution.py:109
  132.2 0.6 copy-start.6
  133.7 25.9 %copy-start.5 = (f32[64,640]{1,0:T(8,128)S(1)}, f32[64,640]{1,0:T(8,128)}, u32[]{:S(2)}) copy-start(f32[64,640]{1,0:T(8,128)} %reduce-scatter.7.cloned.1.call-done) | copy-start | bytes 491524
  136.2 179.7 %all-reduce.3.cloned.1.call-start = ((), (), s32[]{:S(2)}) async-start(), calls=%async_computation.8 | async-start | bytes 1048576 | tf_op jit(solution)/shard_map/psum | solution.py:120
  137.4 21.0 %copy-start.2 = (f32[256,256]{1,0:T(8,128)}, f32[256,256]{1,0:T(8,128)S(1)}, u32[]{:S(2)}) copy-start(f32[256,256]{1,0:T(8,128)S(1)} %fusion.8) | copy-start | bytes 786436
  155.1 164.7 %copy-start.8 = (bf16[128,256]{1,0:T(8,128)(2,1)}, bf16[128,256]{1,0:T(8,128)(2,1)S(1)}, u32[]{:S(2)}) copy-start(bf16[128,256]{1,0:T(8,128)(2,1)S(1)} %convert_element_type.27) | copy-start | bytes 196612
Sparse Core Ops, SparseCore 0:
  55.8 34.1 reduce-scatter.4
  92.8 26.3 reduce-scatter.6
  121.5 32.5 reduce-scatter.8
  156.9 23.7 reduce-scatter.10
  186.5 129.3 all-reduce.2
where the time goes:
time: 327 us; the launch traced here: 326 us
  waiting for transfers between devices  171 us (52%)
  blocking collectives  53.1 us (16%)
  local copies, waits for them, and re-layouts  46.9 us (14%)
  other arithmetic  24.2 us (7%)
  matrix products  16.9 us (5%)
  between operations  14.1 us (4%)
    psum x1, waiting for transfers between devices, on_device(): lax.psum((first_part, second_part + extra_part), ('row', 'col'))  134 us
    reduce_scatter x1, waiting for transfers between devices, on_device(): lax.psum_scatter(-(direct + shifted_part), 'row', scatter_dimension=0, ti...  20.3 us
    all_gather x1, blocking collectives, on_device(): lax.all_gather(take_cols(upper_one, row_one), 'col', axis=0, tiled=True)  17.9 us
    reduce_scatter x1, waiting for transfers between devices, on_device(): lax.psum_scatter(-(direct + shifted_part), 'col', scatter_dimension=0, ti...  16.5 us
    gather x4, local copies, waits for them, and re-layouts, take_rows(): jnp.take(shaped, blocks, axis=0)  16.5 us
    all_gather x1, blocking collectives, on_device(): lax.all_gather(take_cols(upper_two, row_two), 'col', axis=0, tiled=True)  14.9 us
    unnamed x24, local copies, waits for them, and re-layouts  13.7 us
    gather x7, local copies, waits for them, and re-layouts, take_cols(): jnp.take(shaped, blocks, axis=1)  13.3 us
  transfers between devices with their start and end apart: 5, of which 3 were waited for; matrix products, arithmetic and copies ran while one was open for 14% of the time, Pallas kernels for 0%

commit v1 on v0

--- a/solution.py
+++ b/solution.py
@@ -80,7 +80,15 @@
     upper_spots = places(col_two, col_one)
     corner_mine = lax.dynamic_slice_in_dim(corner_upper, row_index * upper_rows, upper_rows, 1)
     lower_p = lax.all_gather(take_rows(lower_one, col_one), "row", axis=1, tiled=True)
-    upper_p = lax.all_gather(take_cols(upper_one, row_one), "col", axis=0, tiled=True)
+    array = take_cols(upper_one, row_one)
+    ways = lax.axis_size("col")
+    pieces = [array]
+    for far in range(1, ways):
+        pieces.append(
+            lax.ppermute(pieces[far - 1], "col", [(d, (d - 1) % ways) for d in range(ways)])
+        )
+    line = jnp.concatenate(pieces, axis=0)
+    upper_p = jnp.roll(line, lax.axis_index("col") * array.shape[0], axis=0)
     inv_lower_one = lax.psum_scatter(
         -jnp.dot(sep_one, lower_p, preferred_element_type=jnp.float32),
         "col",

time: 327 us -> 345 us (1.055)
  waiting for transfers between devices: 171 us -> 193 us
  starting transfers between devices: 0.39 us -> 21.8 us
  blocking collectives: 53.1 us -> 35 us
  matrix products: 16.9 us -> 12.7 us
    ppermute x0 -> x7, starting transfers between devices: none -> 21.6 us  [on_device(): lax.ppermute(pieces[far - 1], 'col', [(d, (d - 1) % ways) for d in range(...]
    all_gather x1 -> x0, blocking collectives: 17.9 us -> none  [on_device(): lax.all_gather(take_cols(upper_one, row_one), 'col', axis=0, tiled=True)]
    ppermute x0 -> x7, waiting for transfers between devices: none -> 12.3 us  [on_device(): lax.ppermute(pieces[far - 1], 'col', [(d, (d - 1) % ways) for d in range(...]
    reduce_scatter x1, waiting for transfers between devices: 16.5 us -> 24.2 us  [on_device(): lax.psum_scatter(-(direct + shifted_part), 'col', scatter_dimension=0, ti...]
    unnamed x24 -> x46, local copies, waits for them, and re-layouts: 13.7 us -> 14.6 us
  transfers between devices with their start and end apart: 5 -> 12, of which waited for: 3 -> 9; matrix products, arithmetic and copies ran while one was open for 14% -> 13% of each run, Pallas kernels for 0% -> 0%
where the time goes in v1:
time: 345 us
  waiting for transfers between devices  193 us (56%)
  local copies, waits for them, and re-layouts  44.2 us (13%)
  blocking collectives  35 us (10%)
  other arithmetic  23.7 us (7%)
  starting transfers between devices  21.8 us (6%)
  between operations  14.3 us (4%)
  matrix products  12.7 us (4%)
    psum x1, waiting for transfers between devices, on_device(): lax.psum((first_part, second_part + extra_part), ('row', 'col'))  134 us
    reduce_scatter x1, waiting for transfers between devices, on_device(): lax.psum_scatter(-(direct + shifted_part), 'col', scatter_dimension=0, ti...  24.2 us
    reduce_scatter x1, waiting for transfers between devices, on_device(): lax.psum_scatter(-(direct + shifted_part), 'row', scatter_dimension=0, ti...  22.6 us
    ppermute x7, starting transfers between devices, on_device(): lax.ppermute(pieces[far - 1], 'col', [(d, (d - 1) % ways) for d in range(...  21.6 us
    gather x4, local copies, waits for them, and re-layouts, take_rows(): jnp.take(shaped, blocks, axis=0)  16.6 us
    all_gather x1, blocking collectives, on_device(): lax.all_gather(take_cols(upper_two, row_two), 'col', axis=0, tiled=True)  14.8 us
    unnamed x46, local copies, waits for them, and re-layouts  14.6 us
    select_n x6, other arithmetic, take_rows(): jnp.take(shaped, blocks, axis=0)  12.4 us
  transfers between devices with their start and end apart: 12, of which 9 were waited for; matrix products, arithmetic and copies ran while one was open for 13% of the time, Pallas kernels for 0%

profile of v1, /device:TPU:0, one launch (start us, length us, event | category | flops | bytes accessed | tf_op | source)
XLA Modules:
  0.0 344.5 jit_solution(16373712340464076776)
XLA Ops:
  8.8 8.9 %gather_fusion = bf16[10,128,3072]{2,1,0:T(8,128)(2,1)} fusion(bf16[48,128,3072]{2,1,0:T(8,128)(2,1)} %bitcast.126, s32[1024]{0:T(1024)S(1)} %get-tuple-element.21), kind=kCustom, calls=%fused_computation | custom fusion | bytes 15728680 | tf_op jit(solution)/shard_map/jit(_take)/gather | solution.py:19
  17.7 5.2 %copy.69 = bf16[160,8,24,128]{3,2,1,0:T(8,128)(2,1)S(1)} copy(bf16[160,8,24,128]{3,1,2,0:T(8,128)(2,1)} %bitcast.121) | data formatting | bytes 15728640
  23.0 5.3 %copy_select_fusion = bf16[1280,24,128]{2,0,1:T(8,128)(2,1)} fusion(bf16[1280,24,128]{2,1,0:T(8,128)(2,1)S(1)} %bitcast.122, pred[1280]{0:T(1024)(128)(4,1)S(1)} %broadcast_bitcast_fusion), kind=kLoop, calls=%fused_computation.9 | loop fusion | flops 3932160 | bytes 15729920 | tf_op jit(solution)/shard_map/jit(_take)/select_n | solution.py:19
  28.2 4.1 %gather_fusion.1 = bf16[5,1280,128]{2,1,0:T(8,128)(2,1)S(1)} fusion(bf16[1280,24,128]{2,0,1:T(8,128)(2,1)} %copy_select_fusion, s32[1024]{0:T(1024)S(1)} %get-tuple-element.20), kind=kCustom, calls=%fused_computation.1 | custom fusion | bytes 3276820 | tf_op jit(solution)/shard_map/jit(_take)/gather | solution.py:24
  32.3 2.4 copy.42
  37.2 11.0 %all_gather.9 = bf16[640,256]{0,1:T(8,128)(2,1)S(1)} all-gather(bf16[640,64]{0,1:T(8,128)(2,1)S(1)} %bitcast_select_fusion.3), channel_id=1, replica_groups=mesh['row'=4,'col'=8] {'row'}, dimensions={1}, use_global_device_ids=true | all-gather | bytes 409600 | tf_op jit(solution)/shard_map/all_gather | solution.py:82
  53.8 6.5 %gather_fusion.4 = bf16[8,128,3072]{2,1,0:T(8,128)(2,1)} fusion(bf16[48,128,3072]{2,1,0:T(8,128)(2,1)} %bitcast.127, s32[1024]{0:T(1024)S(1)} %pad_clamp_fusion.2), kind=kCustom, calls=%fused_computation.4 | custom fusion | bytes 12582944 | tf_op jit(solution)/shard_map/jit(_take)/gather | solution.py:19
  60.3 7.4 %copy.70 = bf16[128,8,24,128]{3,2,1,0:T(8,128)(2,1)} copy(bf16[128,8,24,128]{3,1,2,0:T(8,128)(2,1)} %bitcast.124) | data formatting | bytes 12582912
  68.1 7.1 %copy_select_fusion.1 = bf16[1024,24,128]{2,0,1:T(8,128)(2,1)} fusion(bf16[1024,24,128]{2,1,0:T(8,128)(2,1)} %bitcast.123, pred[1024]{0:T(1024)(128)(4,1)S(1)} %broadcast_bitcast_fusion.1), kind=kLoop, calls=%fused_computation.10 | loop fusion | flops 3145728 | bytes 12583936 | tf_op jit(solution)/shard_map/jit(_take)/select_n | solution.py:19
  75.8 2.5 collective-permute-start.1
  78.3 2.1 collective-permute-done.1
  80.3 3.6 %collective-permute-start.2 = (bf16[32,1280]{1,0:T(8,128)(2,1)S(1)}, bf16[32,1280]{1,0:T(8,128)(2,1)S(1)}, u32[]{:S(2)}, u32[]{:S(2)}) collective-permute-start(bf16[32,1280]{1,0:T(8,128)(2,1)S(1)} %collective-permute-done.1), channel_id=1, source_target_pairs={{0,7},{1,0},{2,1},{3,2},{4,3},{5,4},{6,5},{7,6},{8,15},{9,8},{10,9... | collective-permute-start | bytes 245768 | tf_op jit(solution)/shard_map/ppermute | solution.py:88
  86.0 3.6 %collective-permute-start.3 = (bf16[32,1280]{1,0:T(8,128)(2,1)S(1)}, bf16[32,1280]{1,0:T(8,128)(2,1)S(1)}, u32[]{:S(2)}, u32[]{:S(2)}) collective-permute-start(bf16[32,1280]{1,0:T(8,128)(2,1)S(1)} %collective-permute-done.2), channel_id=1, source_target_pairs={{0,7},{1,0},{2,1},{3,2},{4,3},{5,4},{6,5},{7,6},{8,15},{9,8},{10,9... | collective-permute-start | bytes 245768 | tf_op jit(solution)/shard_map/ppermute | solution.py:88
  91.7 3.6 %collective-permute-start.4 = (bf16[32,1280]{1,0:T(8,128)(2,1)S(1)}, bf16[32,1280]{1,0:T(8,128)(2,1)S(1)}, u32[]{:S(2)}, u32[]{:S(2)}) collective-permute-start(bf16[32,1280]{1,0:T(8,128)(2,1)S(1)} %collective-permute-done.3), channel_id=1, source_target_pairs={{0,7},{1,0},{2,1},{3,2},{4,3},{5,4},{6,5},{7,6},{8,15},{9,8},{10,9... | collective-permute-start | bytes 245768 | tf_op jit(solution)/shard_map/ppermute | solution.py:88
  95.3 2.1 collective-permute-done.4
  97.3 3.6 %collective-permute-start.5 = (bf16[32,1280]{1,0:T(8,128)(2,1)S(1)}, bf16[32,1280]{1,0:T(8,128)(2,1)S(1)}, u32[]{:S(2)}, u32[]{:S(2)}) collective-permute-start(bf16[32,1280]{1,0:T(8,128)(2,1)S(1)} %collective-permute-done.4), channel_id=1, source_target_pairs={{0,7},{1,0},{2,1},{3,2},{4,3},{5,4},{6,5},{7,6},{8,15},{9,8},{10,9... | collective-permute-start | bytes 245768 | tf_op jit(solution)/shard_map/ppermute | solution.py:88
  100.9 2.1 collective-permute-done.5
  103.0 3.6 %collective-permute-start.6 = (bf16[32,1280]{1,0:T(8,128)(2,1)S(1)}, bf16[32,1280]{1,0:T(8,128)(2,1)S(1)}, u32[]{:S(2)}, u32[]{:S(2)}) collective-permute-start(bf16[32,1280]{1,0:T(8,128)(2,1)S(1)} %collective-permute-done.5), channel_id=1, source_target_pairs={{0,7},{1,0},{2,1},{3,2},{4,3},{5,4},{6,5},{7,6},{8,15},{9,8},{10,9... | collective-permute-start | bytes 245768 | tf_op jit(solution)/shard_map/ppermute | solution.py:88
  111.4 9.3 %all_gather.10 = bf16[512,256]{0,1:T(8,128)(2,1)S(1)} all-gather(bf16[512,64]{0,1:T(8,128)(2,1)S(1)} %bitcast_select_fusion.6), channel_id=1, replica_groups=mesh['row'=4,'col'=8] {'row'}, dimensions={1}, use_global_device_ids=true | all-gather | bytes 327680 | tf_op jit(solution)/shard_map/all_gather | solution.py:104
  120.6 3.6 %gather_fusion.5 = bf16[4,1024,128]{2,1,0:T(8,128)(2,1)S(1)} fusion(bf16[1024,24,128]{2,0,1:T(8,128)(2,1)} %copy_select_fusion.1, s32[1024]{0:T(1024)S(1)} %get-tuple-element.19), kind=kCustom, calls=%fused_computation.5 | custom fusion | bytes 2097168 | tf_op jit(solution)/shard_map/jit(_take)/gather | solution.py:24
  129.2 14.8 %all_gather.11 = bf16[256,1024]{1,0:T(8,128)(2,1)S(1)} all-gather(bf16[32,1024]{1,0:T(8,128)(2,1)S(1)} %bitcast_select_fusion.5), channel_id=1, replica_groups=mesh['row'=4,'col'=8] {'col'}, dimensions={0}, use_global_device_ids=true | all-gather | bytes 589824 | tf_op jit(solution)/shard_map/all_gather | solution.py:105
  148.9 24.2 %reduce-scatter.9.cloned.1.call-done = f32[128,256]{1,0:T(8,128)} async-done(((f32[1024,256]{1,0:T(8,128)}), f32[128,256]{1,0:T(8,128)}) %reduce-scatter.9.cloned.1.call-update) | async-done | bytes 131088 | tf_op jit(solution)/shard_map/reduce_scatter | solution.py:111
  176.5 22.6 %reduce-scatter.11.cloned.1.call-done = f32[64,512]{1,0:T(8,128)} async-done(((f32[256,512]{1,0:T(8,128)}), f32[64,512]{1,0:T(8,128)}) %reduce-scatter.11.cloned.1.call-update) | async-done | bytes 131088 | tf_op jit(solution)/shard_map/reduce_scatter | solution.py:117
  200.6 133.7 %all-reduce.3.cloned.1.call-done = (f32[256,256]{1,0:T(8,128)}, f32[256,256]{1,0:T(8,128)}) async-done(((f32[256,256]{1,0:T(8,128)}, f32[256,256]{1,0:T(8,128)}), (f32[256,256]{1,0:T(8,128)}, f32[256,256]{1,0:T(8,128)})) %all-reduce.3.cloned.1.call-update) | async-done | bytes 524304 | tf_op jit(solution)/shard_map/psum | solution.py:128
  (122 shorter events, 37.6 us)
Async XLA Ops:
  7.2 27.6 %copy-start = (bf16[3072,64]{0,1:T(8,128)(2,1)S(1)}, bf16[3072,64]{0,1:T(8,128)(2,1)}, u32[]{:S(2)}) copy-start(bf16[3072,64]{0,1:T(8,128)(2,1)} %param.12) | copy-start | bytes 1179652
  7.2 118.4 %reduce-scatter.5.cloned.1.call-start = ((), (), s32[]{:S(2)}) async-start(), calls=%async_computation.4 | async-start | bytes 1474560 | tf_op jit(solution)/shard_map/reduce_scatter | solution.py:92
  49.9 3.3 copy-start.14
  49.9 94.1 %reduce-scatter.7.cloned.1.call-start = ((), (), s32[]{:S(2)}) async-start(), calls=%async_computation.5 | async-start | bytes 819200 | tf_op jit(solution)/shard_map/reduce_scatter | solution.py:98
  52.2 23.5 %collective-permute-start = (bf16[32,1280]{1,0:T(8,128)(2,1)}, bf16[32,1280]{1,0:T(8,128)(2,1)S(1)}, u32[]{:S(2)}, u32[]{:S(2)}) collective-permute-start(bf16[32,1280]{1,0:T(8,128)(2,1)} %get-tuple-element.13), channel_id=1, source_target_pairs={{0,7},{1,0},{2,1},{3,2},{4,3},{5,4},{6,5},{7,6},{8,15},{9,8},{10,9... | collective-permute-start | bytes 245768 | tf_op jit(solution)/shard_map/ppermute | solution.py:88
  60.3 7.6 %copy-start.10 = (bf16[3072,64]{0,1:T(8,128)(2,1)S(1)}, bf16[3072,64]{0,1:T(8,128)(2,1)}, u32[]{:S(2)}) copy-start(bf16[3072,64]{0,1:T(8,128)(2,1)} %param.16) | copy-start | bytes 1179652
  75.8 4.6 %collective-permute-start.1 = (bf16[32,1280]{1,0:T(8,128)(2,1)S(1)}, bf16[32,1280]{1,0:T(8,128)(2,1)S(1)}, u32[]{:S(2)}, u32[]{:S(2)}) collective-permute-start(bf16[32,1280]{1,0:T(8,128)(2,1)S(1)} %collective-permute-done), channel_id=1, source_target_pairs={{0,7},{1,0},{2,1},{3,2},{4,3},{5,4},{6,5},{7,6},{8,15},{9,8},{10,9... | collective-permute-start | bytes 245768 | tf_op jit(solution)/shard_map/ppermute | solution.py:88
  80.3 5.7 %collective-permute-start.2 = (bf16[32,1280]{1,0:T(8,128)(2,1)S(1)}, bf16[32,1280]{1,0:T(8,128)(2,1)S(1)}, u32[]{:S(2)}, u32[]{:S(2)}) collective-permute-start(bf16[32,1280]{1,0:T(8,128)(2,1)S(1)} %collective-permute-done.1), channel_id=1, source_target_pairs={{0,7},{1,0},{2,1},{3,2},{4,3},{5,4},{6,5},{7,6},{8,15},{9,8},{10,9... | collective-permute-start | bytes 245768 | tf_op jit(solution)/shard_map/ppermute | solution.py:88
  86.0 5.7 %collective-permute-start.3 = (bf16[32,1280]{1,0:T(8,128)(2,1)S(1)}, bf16[32,1280]{1,0:T(8,128)(2,1)S(1)}, u32[]{:S(2)}, u32[]{:S(2)}) collective-permute-start(bf16[32,1280]{1,0:T(8,128)(2,1)S(1)} %collective-permute-done.2), channel_id=1, source_target_pairs={{0,7},{1,0},{2,1},{3,2},{4,3},{5,4},{6,5},{7,6},{8,15},{9,8},{10,9... | collective-permute-start | bytes 245768 | tf_op jit(solution)/shard_map/ppermute | solution.py:88
  91.7 5.7 %collective-permute-start.4 = (bf16[32,1280]{1,0:T(8,128)(2,1)S(1)}, bf16[32,1280]{1,0:T(8,128)(2,1)S(1)}, u32[]{:S(2)}, u32[]{:S(2)}) collective-permute-start(bf16[32,1280]{1,0:T(8,128)(2,1)S(1)} %collective-permute-done.3), channel_id=1, source_target_pairs={{0,7},{1,0},{2,1},{3,2},{4,3},{5,4},{6,5},{7,6},{8,15},{9,8},{10,9... | collective-permute-start | bytes 245768 | tf_op jit(solution)/shard_map/ppermute | solution.py:88
  97.3 5.7 %collective-permute-start.5 = (bf16[32,1280]{1,0:T(8,128)(2,1)S(1)}, bf16[32,1280]{1,0:T(8,128)(2,1)S(1)}, u32[]{:S(2)}, u32[]{:S(2)}) collective-permute-start(bf16[32,1280]{1,0:T(8,128)(2,1)S(1)} %collective-permute-done.4), channel_id=1, source_target_pairs={{0,7},{1,0},{2,1},{3,2},{4,3},{5,4},{6,5},{7,6},{8,15},{9,8},{10,9... | collective-permute-start | bytes 245768 | tf_op jit(solution)/shard_map/ppermute | solution.py:88
  103.0 5.7 %collective-permute-start.6 = (bf16[32,1280]{1,0:T(8,128)(2,1)S(1)}, bf16[32,1280]{1,0:T(8,128)(2,1)S(1)}, u32[]{:S(2)}, u32[]{:S(2)}) collective-permute-start(bf16[32,1280]{1,0:T(8,128)(2,1)S(1)} %collective-permute-done.5), channel_id=1, source_target_pairs={{0,7},{1,0},{2,1},{3,2},{4,3},{5,4},{6,5},{7,6},{8,15},{9,8},{10,9... | collective-permute-start | bytes 245768 | tf_op jit(solution)/shard_map/ppermute | solution.py:88
  111.3 61.7 %reduce-scatter.9.cloned.1.call-start = ((), (), s32[]{:S(2)}) async-start(), calls=%async_computation.6 | async-start | bytes 1179648 | tf_op jit(solution)/shard_map/reduce_scatter | solution.py:111
  126.5 20.9 %copy-start.6 = (bf16[160,256]{1,0:T(8,128)(2,1)}, bf16[160,256]{1,0:T(8,128)(2,1)S(1)}, u32[]{:S(2)}) copy-start(bf16[160,256]{1,0:T(8,128)(2,1)S(1)} %convert_element_type.24) | copy-start | bytes 245764
  126.7 1.7 copy-start.11
  128.4 17.4 %copy-start.4 = (bf16[256,256]{1,0:T(8,128)(2,1)S(1)}, bf16[256,256]{1,0:T(8,128)(2,1)}, u32[]{:S(2)}) copy-start(bf16[256,256]{1,0:T(8,128)(2,1)} %param.19) | copy-start | bytes 393220
  128.4 70.7 %reduce-scatter.11.cloned.1.call-start = ((), (), s32[]{:S(2)}) async-start(), calls=%async_computation.7 | async-start | bytes 655360 | tf_op jit(solution)/shard_map/reduce_scatter | solution.py:117
  147.3 187.0 %all-reduce.3.cloned.1.call-start = ((), (), s32[]{:S(2)}) async-start(), calls=%async_computation.8 | async-start | bytes 1048576 | tf_op jit(solution)/shard_map/psum | solution.py:128
  148.6 26.9 %copy-start.2 = (f32[256,256]{1,0:T(8,128)}, f32[256,256]{1,0:T(8,128)S(1)}, u32[]{:S(2)}) copy-start(f32[256,256]{1,0:T(8,128)S(1)} %fusion.9) | copy-start | bytes 786436
  148.9 26.6 %copy-start.5 = (f32[256,256]{1,0:T(8,128)S(1)}, f32[256,256]{1,0:T(8,128)}, u32[]{:S(2)}) copy-start(f32[256,256]{1,0:T(8,128)} %param.14) | copy-start | bytes 786436
  173.9 1.9 copy-start.12
  174.1 1.7 copy-start.7
  175.5 160.5 %copy-start.13 = (f32[256,256]{1,0:T(8,128)S(1)}, f32[256,256]{1,0:T(8,128)}, u32[]{:S(2)}) copy-start(f32[256,256]{1,0:T(8,128)} %param.20) | copy-start | bytes 786436
  175.5 162.5 %copy-start.1 = (bf16[3072,64]{0,1:T(8,128)(2,1)S(1)}, bf16[3072,64]{0,1:T(8,128)(2,1)}, u32[]{:S(2)}) copy-start(bf16[3072,64]{0,1:T(8,128)(2,1)} %param.12) | copy-start | bytes 1179652
  (3 other events, 4.1 us)
Sparse Core Ops, SparseCore 0:
  50.1 33.5 reduce-scatter.4
  111.4 26.6 reduce-scatter.6
  140.4 32.6 reduce-scatter.8
  175.7 23.2 reduce-scatter.10
  204.9 129.3 all-reduce.2
